TPU v7x, 32 devices: a whole 2x2x4 slice. The times are simulated.
32 devices in a mesh: tile: 16 (over z, x, core), rep: 2 (over y).
Axes of the slice: x: 2, y: 2, z: 4, core: 2. Of those that a mesh axis runs over, the one named last changes fastest.
Arguments:
- waves: bfloat16 [2, 8192, 128], P('rep', 'tile'), may hold values from -6 to 6
- dest_tile: int32 [2, 8192, 1], P('rep', 'tile'), may hold values from 0 to 15; in each aligned block of 512 rows (0 to 511, 512 to 1023, ..., all dimensions but the last counted through in order) at most 32 rows name the same one
- pixel_bin: int32 [2, 8192], P('rep', 'tile'), may hold values from 0 to 1023
- target: float32 [2, 128, 128], P('rep', 'tile'), may hold values from -6 to 6
- conv_one: bfloat16 [3, 3, 128, 128], replicated, may hold values from -0.1875 to 0.1875
- bias_one: float32 [128], replicated, may hold values from -0.5 to 0.5
- conv_two: bfloat16 [3, 3, 128], replicated, may hold values from -0.1875 to 0.1875
- bias_two: float32 [1], replicated, may hold values from -1 to 1
Outputs:
- prediction: float32 [2, 128, 128], P('rep', 'tile')
- update_one: float32 [3, 3, 128, 128], replicated
- update_bias: float32 [128], replicated
- update_two: float32 [3, 3, 128], replicated
Inputs may be any that keep to these rules, and one draw needn't show every extreme that they name: `dest_tile`: among the rows of one device, no strip is named more than 32 times, a bound that some block reaches.
All inputs are finite; a program needn't handle non-finite values.
Results may differ from a plain program's by a relative error of at most 0.0024.
The roundings to bfloat16 on the way count: a program that leaves them out, or rounds other values in their place, can miss the bound.
Values may be sent and summed in bfloat16 or wider, within the bound.
A program may use at most 64 MiB of HBM per device.

v0:
```python
import math
import jax
import jax.numpy as jnp
from jax import lax
from jax.sharding import PartitionSpec as P

CAP = 32


def extended(block, sides, width):
    for axis, dim in sides:
        count = lax.axis_size(axis)
        forward = [(i, i + 1) for i in range(count - 1)]
        backward = [(target, source) for source, target in forward]
        low = lax.ppermute(
            lax.slice_in_dim(block, block.shape[dim] - width, None, axis=dim), axis, forward
        )
        high = lax.ppermute(lax.slice_in_dim(block, 0, width, axis=dim), axis, backward)
        block = jnp.concatenate([low, block, high], axis=dim)
    return block


def normalized(grad):
    return grad / jnp.sqrt(jnp.mean(grad * grad) + 1e-06)


def first_conv(padded, conv_one, bias_one, tall, width):
    steps = padded.shape[2]
    channels = conv_one.shape[3]
    pre = jnp.zeros((tall * width, channels), jnp.float32) + bias_one[None, :]
    for i in range(3):
        for j in range(3):
            patch = padded[2 * i : 2 * i + tall, 2 * j : 2 * j + width, :].reshape(
                tall * width, steps
            )
            pre = pre + jnp.dot(patch, conv_one[i, j], preferred_element_type=jnp.float32)
    return pre.reshape(tall, width, channels)


def second_conv(hidden_pad, conv_two, bias_two, tall, width):
    pred = jnp.zeros((tall, width), jnp.float32) + bias_two[0]
    for i in range(3):
        for j in range(3):
            pred = pred + jnp.einsum(
                "hwc,c->hw",
                hidden_pad[i : i + tall, j : j + width, :],
                conv_two[i, j],
                preferred_element_type=jnp.float32,
            )
    return pred


def on_device(waves, dest_tile, pixel_bin, target, conv_one, bias_one, conv_two, bias_two):
    tiles = lax.axis_size("tile")
    replicas = lax.axis_size("rep")
    steps = waves.shape[2]
    height = target.shape[1]
    width = target.shape[2]
    pixels = height * width
    channels = conv_one.shape[3]
    bucket = CAP
    tile_ids = dest_tile[0, :, 0]
    hits = (tile_ids[:, None] == jnp.arange(tiles, dtype=jnp.int32)[None, :]).astype(jnp.int32)
    rank = jnp.sum(jnp.cumsum(hits, axis=0) * hits, axis=1) - 1
    slots = tile_ids * bucket + rank
    send_wave = jnp.zeros((tiles * bucket, steps), jnp.bfloat16).at[slots].set(waves[0])
    send_bin = jnp.full((tiles * bucket,), -1, jnp.int32).at[slots].set(pixel_bin[0])
    recv_wave, recv_bin = (
        lax.all_to_all(
            send_wave.reshape(tiles, bucket, steps), "tile", split_axis=0, concat_axis=0, tiled=True
        ),
        lax.all_to_all(
            send_bin.reshape(tiles, bucket), "tile", split_axis=0, concat_axis=0, tiled=True
        ),
    )
    recv_wave = recv_wave.reshape(tiles * bucket, steps)
    recv_bin = recv_bin.reshape(tiles * bucket)
    block = math.gcd(pixels, 128)

    def raster(start):
        wanted = start + jnp.arange(block, dtype=jnp.int32)
        onehot = (wanted[:, None] == recv_bin[None, :]).astype(jnp.bfloat16)
        return jnp.dot(onehot, recv_wave, preferred_element_type=jnp.float32).astype(jnp.bfloat16)

    starts = jnp.arange(0, pixels, block, dtype=jnp.int32)
    grid = lax.map(raster, starts)
    padded = extended(grid, (("tile", 0),), 2)
    padded = jnp.pad(padded, ((0, 0), (2, 2), (0, 0)))
    pre = first_conv(padded, conv_one, bias_one, height, width)
    hidden = jax.nn.silu(pre).astype(jnp.bfloat16)
    hidden_pad = extended(hidden, (("tile", 0),), 1)
    hidden_pad = jnp.pad(hidden_pad, ((0, 0), (1, 1), (0, 0)))
    pred = second_conv(hidden_pad, conv_two, bias_two, height, width)
    error = ((pred - target[0]) / replicas).astype(jnp.bfloat16)
    error_pad = extended(error, (("tile", 0),), 1)
    error_pad = jnp.pad(error_pad, ((0, 0), (1, 1)))
    grad_two = []
    back = jnp.zeros((height, width, channels), jnp.float32)
    for i in range(3):
        for j in range(3):
            grad_two.append(
                jnp.einsum(
                    "hwc,hw->c",
                    hidden_pad[i : i + height, j : j + width, :],
                    error,
                    preferred_element_type=jnp.float32,
                )
            )
            shifted = error_pad[2 - i : 2 - i + height, 2 - j : 2 - j + width].astype(jnp.float32)
            back = back + shifted[:, :, None] * conv_two[i, j].astype(jnp.float32)[None, None, :]
    grad_two = jnp.stack(grad_two).reshape(3, 3, channels)
    sig = jax.nn.sigmoid(pre)
    slope = (back * sig * (1.0 + pre * (1.0 - sig))).astype(jnp.bfloat16)
    slope_flat = slope.reshape(pixels, channels)
    grad_one = []
    for i in range(3):
        for j in range(3):
            patch = padded[2 * i : 2 * i + height, 2 * j : 2 * j + width, :].reshape(pixels, steps)
            grad_one.append(
                lax.dot_general(
                    patch, slope_flat, (((0,), (0,)), ((), ())), preferred_element_type=jnp.float32
                )
            )
    grad_one = jnp.stack(grad_one).reshape(3, 3, steps, channels)
    grad_bias = jnp.sum(slope_flat.astype(jnp.float32), axis=0)
    share = lax.psum_scatter(
        grad_one.reshape(9 * steps, channels), "tile", scatter_dimension=0, tiled=True
    )
    share = lax.psum(share, "rep")
    grad_one = lax.all_gather(share, "tile", axis=0, tiled=True).reshape(3, 3, steps, channels)
    grad_bias, grad_two = lax.psum((grad_bias, grad_two), ("tile", "rep"))
    return (pred[None], normalized(grad_one), normalized(grad_bias), normalized(grad_two))


def solution(mesh):
    placed = (
        P("rep", "tile", None),
        P("rep", "tile", None),
        P("rep", "tile"),
        P("rep", "tile", None),
        P(),
        P(),
        P(),
        P(),
    )
    return jax.shard_map(
        on_device,
        mesh=mesh,
        in_specs=placed,
        out_specs=(P("rep", "tile", None), P(), P(), P()),
        check_vma=False,
    )
```

profile of v0, /device:TPU:0, one launch (start us, length us, event | category | flops | bytes accessed | tf_op | source)
XLA Modules:
  0.0 186.0 jit_solution(650408584183058171)
XLA Ops:
  7.2 0.7 fusion.75
  7.9 1.1 reduce-window.6
  9.3 0.8 fusion.56
  10.1 0.7 compare_select_fusion
  10.8 2.6 %scatter_custom_fusion = s32[512]{0:T(512)S(1)} fusion(s32[512]{0:T(512)S(1)} %bitcast.330, s32[512]{0:T(512)} %bitcast.332, s32[]{:T(128)} %constant.22.clone.1), kind=kCustom, calls=%fused_computation.156 | custom fusion | bytes 2560 | tf_op jit(solution)/shard_map/scatter | solution.py:67
  13.4 0.7 all_to_all.11
  14.1 7.4 %all-to-all-start = ((s32[16,1,32]{2,1,0:T(1,128)}), s32[16,1,32]{2,1,0:T(1,128)S(1)}, u32[]{:S(2)}, u32[]{:S(2)}) async-start(s32[16,1,32]{2,1,0:T(1,128)} %all_to_all.11), calls=%async_computation | async-start | bytes 16384 | tf_op jit(solution)/shard_map/all_to_all | solution.py:72
  21.4 2.4 %scatter_custom_fusion.1 = bf16[512,128]{1,0:T(8,128)(2,1)} fusion(s32[512]{0:T(512)S(1)} %bitcast.331, bf16[1,512,128]{2,1,0:T(8,128)(2,1)S(1)} %copy-done, bf16[]{:T(256)} %constant.14.clone.1), kind=kCustom, calls=%fused_computation.100 | custom fusion | bytes 262146 | tf_op jit(solution)/shard_map/scatter | solution.py:66
  23.8 4.0 %all-to-all-done = s32[16,1,32]{2,1,0:T(1,128)S(1)} async-done(((s32[16,1,32]{2,1,0:T(1,128)}), s32[16,1,32]{2,1,0:T(1,128)S(1)}, u32[]{:S(2)}, u32[]{:S(2)}) %all-to-all-start) | async-done | bytes 2080 | tf_op jit(solution)/shard_map/all_to_all | solution.py:72
  27.8 3.5 %all-to-all-start.1 = ((bf16[16,32,128]{2,1,0:T(8,128)(2,1)}), bf16[16,32,128]{2,1,0:T(8,128)(2,1)S(1)}, u32[]{:S(2)}, u32[]{:S(2)}) async-start(bf16[16,32,128]{2,1,0:T(8,128)(2,1)} %bitcast.12), calls=%async_computation.1 | async-start | bytes 262144 | tf_op jit(solution)/shard_map/all_to_all | solution.py:69
  31.5 7.8 %all-to-all-done.1 = bf16[16,32,128]{2,1,0:T(8,128)(2,1)S(1)} async-done(((bf16[16,32,128]{2,1,0:T(8,128)(2,1)}), bf16[16,32,128]{2,1,0:T(8,128)(2,1)S(1)}, u32[]{:S(2)}, u32[]{:S(2)}) %all-to-all-start.1) | async-done | bytes 131104 | tf_op jit(solution)/shard_map/all_to_all | solution.py:69
  39.3 12.0 %while.11 = (s32[]{:T(128)}, bf16[8,128,128]{2,1,0:T(8,128)(2,1)S(1)}, s32[8]{0:T(128)S(1)}, s32[16,32]{1,0:T(8,128)}, bf16[512,128]{1,0:T(8,128)(2,1)S(1)}, /*index=5*/s32[512]{0:T(512)S(1)}, s32[]{:T(128)}) while((s32[]{:T(128)}, bf16[8,128,128]{2,1,0:T(8,128)(2,1)S(1)}, s32[8]{0:T(128)S(1)}, s32[16,32]{1,0:T(8,128)}, ...), condition=%wide.wide.region_6.7_spmd, body=%wide.wide.region_5.6_spmd.sunk | while | flops 16859264 | bytes 167009 | solution.py:86
  39.3 0.6 dynamic_slice.6
  39.8 0.6 iota_add_fusion.3
  40.8 0.6 dynamic_slice.6
  41.4 0.6 iota_add_fusion.3
  42.3 0.6 dynamic_slice.6
  42.9 0.6 iota_add_fusion.3
  43.8 0.6 dynamic_slice.6
  44.4 0.6 iota_add_fusion.3
  45.3 0.6 dynamic_slice.6
  45.9 0.6 iota_add_fusion.3
  46.8 0.6 dynamic_slice.6
  47.4 0.6 iota_add_fusion.3
  48.3 0.6 dynamic_slice.6
  48.9 0.6 iota_add_fusion.3
  49.8 0.6 dynamic_slice.6
  50.4 0.6 iota_add_fusion.3
  51.5 1.3 collective-permute-start
  52.8 1.3 collective-permute-start.1
  54.1 0.6 bitcast_convert_fusion.8
  55.4 0.6 collective-permute-done.1
  56.0 0.6 copy-done.4
  56.7 0.4 fusion.19
  57.0 0.4 fusion.137
  57.6 0.9 pad_maximum_fusion.2
  58.6 0.9 copy.39
  59.4 0.8 copy.40
  61.2 1.0 convolution_add_fusion.8
  62.5 0.7 copy-done.1
  64.5 0.3 multiply_convert_fusion.2
  65.0 4.4 %collective-permute-start.2 = (bf16[1,128,128]{2,1,0:T(8,128)(2,1)S(1)}, bf16[1,128,128]{2,1,0:T(8,128)(2,1)S(1)}, u32[]{:S(2)}, u32[]{:S(2)}) collective-permute-start(bf16[1,128,128]{2,1,0:T(8,128)(2,1)S(1)} %get-tuple-element.53), channel_id=1, source_target_pairs={{0,2},{2,4},{4,6},{6,8},{8,10},{10,12},{12,14},{14,16},{16,18},{18... | collective-permute-start | bytes 98312 | tf_op jit(solution)/shard_map/ppermute | solution.py:15
  69.4 1.3 collective-permute-start.3
  70.8 1.6 collective-permute-done.3
  74.2 0.6 convert_bitcast_fusion
  76.0 4.8 %collective-permute-start.4 = (bf16[1,128]{1,0:T(2,128)(2,1)S(1)}, bf16[1,128]{1,0:T(2,128)(2,1)S(1)}, u32[]{:S(2)}, u32[]{:S(2)}) collective-permute-start(bf16[1,128]{1,0:T(2,128)(2,1)S(1)} %get-tuple-element.87), channel_id=1, source_target_pairs={{0,2},{2,4},{4,6},{6,8},{8,10},{10,12},{12,14},{14,16},{16,18},{18... | collective-permute-start | bytes 776 | tf_op jit(solution)/shard_map/ppermute | solution.py:15
  80.8 1.3 collective-permute-start.5
  82.4 1.4 collective-permute-done.5
  84.0 1.6 multiply_convert_fusion.1
  86.1 0.3 fusion.13
  86.9 0.3 fusion.10
  87.7 0.3 fusion.8
  88.0 0.8 copy-done.3
  88.8 1.6 convert_reduce_fusion
  90.5 42.7 %all-reduce.4 = (f32[128]{0:T(128)S(1)}, f32[3,3,128]{2,1,0:T(4,128)S(1)}) all-reduce(f32[128]{0:T(128)S(1)} %convert_reduce_fusion, f32[3,3,128]{2,1,0:T(4,128)S(1)} %reshape.152), channel_id=1, replica_groups=mesh['tile'=16,'rep'=2] {'tile','rep'}, use_global_device_ids=true, to_apply=%region_11.12 | all-reduce | flops 1280 | bytes 10240 | tf_op jit(solution)/shard_map/psum | solution.py:131
  133.2 0.6 multiply_reduce_fusion.1
  134.4 0.6 multiply_reduce_fusion.2
  135.7 0.5 broadcast_divide_fusion.2
  136.3 0.6 broadcast_divide_fusion.1
  136.9 9.8 %reduce-scatter.4.cloned.1.call-done = f32[72,128]{1,0:T(8,128)} async-done(((f32[1152,128]{1,0:T(8,128)}), f32[72,128]{1,0:T(8,128)}) %reduce-scatter.4.cloned.1.call-update) | async-done | bytes 36880
  146.7 9.1 %psum.21 = f32[72,128]{1,0:T(8,128)S(1)} all-reduce(f32[72,128]{1,0:T(8,128)} %reduce-scatter.4.cloned.1.call-done), channel_id=1, replica_groups=mesh['tile'=16,'rep'=2] {'rep'}, use_global_device_ids=true, to_apply=%region_8.9 | all-reduce | flops 9216 | bytes 73728 | tf_op jit(solution)/shard_map/psum | solution.py:129
  155.8 21.1 %all_gather.3 = f32[1152,128]{1,0:T(8,128)S(1)} all-gather(f32[72,128]{1,0:T(8,128)S(1)} %psum.21), channel_id=1, replica_groups=mesh['tile'=16,'rep'=2] {'tile'}, dimensions={0}, use_global_device_ids=true | all-gather | bytes 626688 | tf_op jit(solution)/shard_map/all_gather | solution.py:130
  176.9 0.7 multiply_reduce_fusion
  178.3 0.9 broadcast_divide_fusion
  (101 shorter events, 10.4 us)
Async XLA Ops:
  7.2 14.3 %copy-start = (bf16[1,512,128]{2,1,0:T(8,128)(2,1)S(1)}, bf16[1,512,128]{2,1,0:T(8,128)(2,1)}, u32[]{:S(2)}) copy-start(bf16[1,512,128]{2,1,0:T(8,128)(2,1)} %param.10) | copy-start | bytes 393220
  14.1 13.8 %all-to-all-start = ((s32[16,1,32]{2,1,0:T(1,128)}), s32[16,1,32]{2,1,0:T(1,128)S(1)}, u32[]{:S(2)}, u32[]{:S(2)}) async-start(s32[16,1,32]{2,1,0:T(1,128)} %all_to_all.11), calls=%async_computation | async-start | bytes 16384 | tf_op jit(solution)/shard_map/all_to_all | solution.py:72
  27.8 11.4 %copy-start.9 = (s32[16,1,32]{2,1,0:T(1,128)}, s32[16,1,32]{2,1,0:T(1,128)S(1)}, u32[]{:S(2)}) copy-start(s32[16,1,32]{2,1,0:T(1,128)S(1)} %all-to-all-done) | copy-start | bytes 6148
  27.8 11.4 %all-to-all-start.1 = ((bf16[16,32,128]{2,1,0:T(8,128)(2,1)}), bf16[16,32,128]{2,1,0:T(8,128)(2,1)S(1)}, u32[]{:S(2)}, u32[]{:S(2)}) async-start(bf16[16,32,128]{2,1,0:T(8,128)(2,1)} %bitcast.12), calls=%async_computation.1 | async-start | bytes 262144 | tf_op jit(solution)/shard_map/all_to_all | solution.py:69
  31.4 115.3 %reduce-scatter.4.cloned.1.call-start = ((), (), s32[]{:S(2)}) async-start(), calls=%async_computation.3 | async-start | bytes 626688
  39.3 14.9 %copy-start.10 = (bf16[3,3,128]{2,1,0:T(4,128)(2,1)S(1)}, bf16[3,3,128]{2,1,0:T(4,128)(2,1)}, u32[]{:S(2)}) copy-start(bf16[3,3,128]{2,1,0:T(4,128)(2,1)} %param.16) | copy-start | bytes 6916
  51.5 3.9 %collective-permute-start = (bf16[2,128,128]{1,2,0:T(8,128)(2,1)S(1)}, bf16[2,128,128]{1,2,0:T(8,128)(2,1)S(1)}, u32[]{:S(2)}, u32[]{:S(2)}) collective-permute-start(bf16[2,128,128]{1,2,0:T(8,128)(2,1)S(1)} %get-tuple-element.57), channel_id=1, source_target_pairs={{0,2},{2,4},{4,6},{6,8},{8,10},{10,12},{12,14},{14,16},{16,18},{18... | collective-permute-start | bytes 196616 | tf_op jit(solution)/shard_map/ppermute | solution.py:15
  52.8 3.1 %collective-permute-start.1 = (bf16[2,128,128]{1,2,0:T(8,128)(2,1)S(1)}, bf16[2,128,128]{1,2,0:T(8,128)(2,1)S(1)}, u32[]{:S(2)}, u32[]{:S(2)}) collective-permute-start(bf16[2,128,128]{1,2,0:T(8,128)(2,1)S(1)} %get-tuple-element.58), channel_id=1, source_target_pairs={{2,0},{4,2},{6,4},{8,6},{10,8},{12,10},{14,12},{16,14},{18,16},{20... | collective-permute-start | bytes 196616 | tf_op jit(solution)/shard_map/ppermute | solution.py:18
  55.4 0.6 copy-start.6
  56.0 0.6 copy-start.4
  61.0 1.3 copy-start.2
  61.2 1.1 copy-start.8
  62.3 1.0 copy-start.1
  65.0 5.9 %collective-permute-start.2 = (bf16[1,128,128]{2,1,0:T(8,128)(2,1)S(1)}, bf16[1,128,128]{2,1,0:T(8,128)(2,1)S(1)}, u32[]{:S(2)}, u32[]{:S(2)}) collective-permute-start(bf16[1,128,128]{2,1,0:T(8,128)(2,1)S(1)} %get-tuple-element.53), channel_id=1, source_target_pairs={{0,2},{2,4},{4,6},{6,8},{8,10},{10,12},{12,14},{14,16},{16,18},{18... | collective-permute-start | bytes 98312 | tf_op jit(solution)/shard_map/ppermute | solution.py:15
  69.4 3.1 %collective-permute-start.3 = (bf16[1,128,128]{2,1,0:T(8,128)(2,1)S(1)}, bf16[1,128,128]{2,1,0:T(8,128)(2,1)S(1)}, u32[]{:S(2)}, u32[]{:S(2)}) collective-permute-start(bf16[1,128,128]{2,1,0:T(8,128)(2,1)S(1)} %get-tuple-element.54), channel_id=1, source_target_pairs={{2,0},{4,2},{6,4},{8,6},{10,8},{12,10},{14,12},{16,14},{18,16},{20... | collective-permute-start | bytes 98312 | tf_op jit(solution)/shard_map/ppermute | solution.py:18
  73.5 0.7 copy-start.17
  75.8 8.2 %copy-start.11 = (f32[128]{0:T(128)S(1)}, f32[128]{0:T(128)}, u32[]{:S(2)}) copy-start(f32[128]{0:T(128)} %get-tuple-element.74) | copy-start | bytes 1540
  75.8 8.2 %copy-start.12 = (f32[128]{0:T(128)S(1)}, f32[128]{0:T(128)}, u32[]{:S(2)}) copy-start(f32[128]{0:T(128)} %get-tuple-element.75) | copy-start | bytes 1540
  75.8 8.2 %copy-start.13 = (f32[128]{0:T(128)S(1)}, f32[128]{0:T(128)}, u32[]{:S(2)}) copy-start(f32[128]{0:T(128)} %get-tuple-element.76) | copy-start | bytes 1540
  75.8 8.2 %copy-start.14 = (f32[128]{0:T(128)S(1)}, f32[128]{0:T(128)}, u32[]{:S(2)}) copy-start(f32[128]{0:T(128)} %get-tuple-element.77) | copy-start | bytes 1540
  75.8 8.2 %copy-start.15 = (f32[128]{0:T(128)S(1)}, f32[128]{0:T(128)}, u32[]{:S(2)}) copy-start(f32[128]{0:T(128)} %get-tuple-element.78) | copy-start | bytes 1540
  75.8 8.2 %copy-start.16 = (f32[128]{0:T(128)S(1)}, f32[128]{0:T(128)}, u32[]{:S(2)}) copy-start(f32[128]{0:T(128)} %get-tuple-element.79) | copy-start | bytes 1540
  76.0 6.5 %collective-permute-start.4 = (bf16[1,128]{1,0:T(2,128)(2,1)S(1)}, bf16[1,128]{1,0:T(2,128)(2,1)S(1)}, u32[]{:S(2)}, u32[]{:S(2)}) collective-permute-start(bf16[1,128]{1,0:T(2,128)(2,1)S(1)} %get-tuple-element.87), channel_id=1, source_target_pairs={{0,2},{2,4},{4,6},{6,8},{8,10},{10,12},{12,14},{14,16},{16,18},{18... | collective-permute-start | bytes 776 | tf_op jit(solution)/shard_map/ppermute | solution.py:15
  80.8 3.0 %collective-permute-start.5 = (bf16[1,128]{1,0:T(2,128)(2,1)S(1)}, bf16[1,128]{1,0:T(2,128)(2,1)S(1)}, u32[]{:S(2)}, u32[]{:S(2)}) collective-permute-start(bf16[1,128]{1,0:T(2,128)(2,1)S(1)} %get-tuple-element.88), channel_id=1, source_target_pairs={{2,0},{4,2},{6,4},{8,6},{10,8},{12,10},{14,12},{16,14},{18,16},{20... | collective-permute-start | bytes 776 | tf_op jit(solution)/shard_map/ppermute | solution.py:18
  82.4 3.5 %copy-start.7 = (bf16[2,128,128]{1,2,0:T(8,128)(2,1)S(1)}, bf16[2,128,128]{1,2,0:T(8,128)(2,1)}, u32[]{:S(2)}) copy-start(bf16[2,128,128]{1,2,0:T(8,128)(2,1)} %copy-done.6) | copy-start | bytes 196612
  86.6 0.8 copy-start.5
  88.0 0.8 copy-start.3
Sparse Core Ops, SparseCore 0:
  88.9 57.6 reduce-scatter.3
where the time goes:
time: 187 us; the launch traced here: 186 us
  blocking collectives  72.9 us (39%)
  starting transfers between devices  25.2 us (13%)
  waiting for transfers between devices  25.2 us (13%)
  other arithmetic  18.6 us (10%)
  between operations  17.3 us (9%)
  local copies, waits for them, and re-layouts  16.5 us (9%)
  matrix products  10.1 us (5%)
    psum x1, blocking collectives, on_device(): grad_bias, grad_two = lax.psum((grad_bias, grad_two), ('tile', 'rep'))  42.7 us
    all_gather x1, blocking collectives, on_device(): lax.all_gather(share, 'tile', axis=0, tiled=True)  21.1 us
    ppermute x3, starting transfers between devices, extended(): lax.ppermute(lax.slice_in_dim(block, block.shape[dim] - width, None, axis...  10.5 us
    unnamed x2, waiting for transfers between devices  9.84 us
    psum x1, blocking collectives, on_device(): share = lax.psum(share, 'rep')  9.1 us
    all_to_all x1, waiting for transfers between devices, on_device(): lax.all_to_all(send_wave.reshape(tiles, bucket, steps), 'tile', split_axi...  7.75 us
    all_to_all x1, starting transfers between devices, on_device(): lax.all_to_all(send_bin.reshape(tiles, bucket), 'tile', split_axis=0, con...  7.36 us
    add x8, other arithmetic, raster(): wanted = start + jnp.arange(block, dtype=jnp.int32)  5.17 us
  transfers between devices with their start and end apart: 9, of which 6 were waited for; matrix products, arithmetic and copies ran while one was open for 4% of the time, Pallas kernels for 0%

commit v1 on v0

--- a/solution.py
+++ b/solution.py
@@ -126,7 +126,13 @@
     share = lax.psum_scatter(
         grad_one.reshape(9 * steps, channels), "tile", scatter_dimension=0, tiled=True
     )
-    share = lax.psum(share, "rep")
+
+    def wrap_the_task(z_in, a_name):
+        h_now = lax.all_gather(z_in, axis_name=a_name)
+        plain = jnp.sum(h_now, axis=0)
+        return plain
+
+    share = wrap_the_task(share, "rep")
     grad_one = lax.all_gather(share, "tile", axis=0, tiled=True).reshape(3, 3, steps, channels)
     grad_bias, grad_two = lax.psum((grad_bias, grad_two), ("tile", "rep"))
     return (pred[None], normalized(grad_one), normalized(grad_bias), normalized(grad_two))

time: 187 us -> 183 us (0.979)
  blocking collectives: 72.9 us -> 68.6 us
    psum x1 -> x0, blocking collectives: 9.1 us -> none  [on_device(): share = lax.psum(share, 'rep')]
    all_gather x0 -> x1, blocking collectives: none -> 4.83 us  [wrap_the_task(): h_now = lax.all_gather(z_in, axis_name=a_name)]
where the time goes in v1:
time: 183 us; the launch traced here: 182 us
  blocking collectives  68.6 us (37%)
  starting transfers between devices  25.2 us (14%)
  waiting for transfers between devices  25.2 us (14%)
  other arithmetic  18.6 us (10%)
  between operations  17.3 us (9%)
  local copies, waits for them, and re-layouts  16.5 us (9%)
  matrix products  10.1 us (6%)
    psum x1, blocking collectives, on_device(): grad_bias, grad_two = lax.psum((grad_bias, grad_two), ('tile', 'rep'))  42.7 us
    all_gather x1, blocking collectives, on_device(): lax.all_gather(share, 'tile', axis=0, tiled=True)  21.1 us
    ppermute x3, starting transfers between devices, extended(): lax.ppermute(lax.slice_in_dim(block, block.shape[dim] - width, None, axis...  10.5 us
    unnamed x2, waiting for transfers between devices  9.84 us
    all_to_all x1, waiting for transfers between devices, on_device(): lax.all_to_all(send_wave.reshape(tiles, bucket, steps), 'tile', split_axi...  7.75 us
    all_to_all x1, starting transfers between devices, on_device(): lax.all_to_all(send_bin.reshape(tiles, bucket), 'tile', split_axis=0, con...  7.36 us
    add x8, other arithmetic, raster(): wanted = start + jnp.arange(block, dtype=jnp.int32)  5.17 us
    all_gather x1, blocking collectives, wrap_the_task(): h_now = lax.all_gather(z_in, axis_name=a_name)  4.83 us
  transfers between devices with their start and end apart: 9, of which 6 were waited for; matrix products, arithmetic and copies ran while one was open for 4% of the time, Pallas kernels for 0%

profile of v1, /device:TPU:0, one launch (start us, length us, event | category | flops | bytes accessed | tf_op | source)
XLA Modules:
  0.0 181.8 jit_solution(10842800331650394176)
XLA Ops:
  7.2 0.7 fusion.75
  7.9 1.1 reduce-window.6
  9.3 0.8 fusion.56
  10.1 0.7 compare_select_fusion
  10.8 2.6 %scatter_custom_fusion = s32[512]{0:T(512)S(1)} fusion(s32[512]{0:T(512)S(1)} %bitcast.332, s32[512]{0:T(512)} %bitcast.334, s32[]{:T(128)} %constant.22.clone.1), kind=kCustom, calls=%fused_computation.156 | custom fusion | bytes 2560 | tf_op jit(solution)/shard_map/scatter | solution.py:67
  13.4 0.7 all_to_all.11
  14.1 7.4 %all-to-all-start = ((s32[16,1,32]{2,1,0:T(1,128)}), s32[16,1,32]{2,1,0:T(1,128)S(1)}, u32[]{:S(2)}, u32[]{:S(2)}) async-start(s32[16,1,32]{2,1,0:T(1,128)} %all_to_all.11), calls=%async_computation | async-start | bytes 16384 | tf_op jit(solution)/shard_map/all_to_all | solution.py:72
  21.4 2.4 %scatter_custom_fusion.1 = bf16[512,128]{1,0:T(8,128)(2,1)} fusion(s32[512]{0:T(512)S(1)} %bitcast.333, bf16[1,512,128]{2,1,0:T(8,128)(2,1)S(1)} %copy-done, bf16[]{:T(256)} %constant.14.clone.1), kind=kCustom, calls=%fused_computation.100 | custom fusion | bytes 262146 | tf_op jit(solution)/shard_map/scatter | solution.py:66
  23.8 4.0 %all-to-all-done = s32[16,1,32]{2,1,0:T(1,128)S(1)} async-done(((s32[16,1,32]{2,1,0:T(1,128)}), s32[16,1,32]{2,1,0:T(1,128)S(1)}, u32[]{:S(2)}, u32[]{:S(2)}) %all-to-all-start) | async-done | bytes 2080 | tf_op jit(solution)/shard_map/all_to_all | solution.py:72
  27.8 3.5 %all-to-all-start.1 = ((bf16[16,32,128]{2,1,0:T(8,128)(2,1)}), bf16[16,32,128]{2,1,0:T(8,128)(2,1)S(1)}, u32[]{:S(2)}, u32[]{:S(2)}) async-start(bf16[16,32,128]{2,1,0:T(8,128)(2,1)} %bitcast.12), calls=%async_computation.1 | async-start | bytes 262144 | tf_op jit(solution)/shard_map/all_to_all | solution.py:69
  31.5 7.8 %all-to-all-done.1 = bf16[16,32,128]{2,1,0:T(8,128)(2,1)S(1)} async-done(((bf16[16,32,128]{2,1,0:T(8,128)(2,1)}), bf16[16,32,128]{2,1,0:T(8,128)(2,1)S(1)}, u32[]{:S(2)}, u32[]{:S(2)}) %all-to-all-start.1) | async-done | bytes 131104 | tf_op jit(solution)/shard_map/all_to_all | solution.py:69
  39.3 12.0 %while.11 = (s32[]{:T(128)}, bf16[8,128,128]{2,1,0:T(8,128)(2,1)S(1)}, s32[8]{0:T(128)S(1)}, s32[16,32]{1,0:T(8,128)}, bf16[512,128]{1,0:T(8,128)(2,1)S(1)}, /*index=5*/s32[512]{0:T(512)S(1)}, s32[]{:T(128)}) while((s32[]{:T(128)}, bf16[8,128,128]{2,1,0:T(8,128)(2,1)S(1)}, s32[8]{0:T(128)S(1)}, s32[16,32]{1,0:T(8,128)}, ...), condition=%wide.wide.region_6.7_spmd, body=%wide.wide.region_5.6_spmd.sunk | while | flops 16859264 | bytes 167009 | solution.py:86
  39.3 0.6 dynamic_slice.6
  39.8 0.6 iota_add_fusion.3
  40.8 0.6 dynamic_slice.6
  41.4 0.6 iota_add_fusion.3
  42.3 0.6 dynamic_slice.6
  42.9 0.6 iota_add_fusion.3
  43.8 0.6 dynamic_slice.6
  44.4 0.6 iota_add_fusion.3
  45.3 0.6 dynamic_slice.6
  45.9 0.6 iota_add_fusion.3
  46.8 0.6 dynamic_slice.6
  47.4 0.6 iota_add_fusion.3
  48.3 0.6 dynamic_slice.6
  48.9 0.6 iota_add_fusion.3
  49.8 0.6 dynamic_slice.6
  50.4 0.6 iota_add_fusion.3
  51.5 1.3 collective-permute-start
  52.8 1.3 collective-permute-start.1
  54.1 0.6 bitcast_convert_fusion.8
  55.4 0.6 collective-permute-done.1
  56.0 0.6 copy-done.4
  56.7 0.4 fusion.19
  57.0 0.4 fusion.137
  57.6 0.9 pad_maximum_fusion.2
  58.6 0.9 copy.39
  59.4 0.8 copy.40
  61.2 1.0 convolution_add_fusion.8
  62.5 0.7 copy-done.1
  64.5 0.3 multiply_convert_fusion.2
  65.0 4.4 %collective-permute-start.2 = (bf16[1,128,128]{2,1,0:T(8,128)(2,1)S(1)}, bf16[1,128,128]{2,1,0:T(8,128)(2,1)S(1)}, u32[]{:S(2)}, u32[]{:S(2)}) collective-permute-start(bf16[1,128,128]{2,1,0:T(8,128)(2,1)S(1)} %get-tuple-element.53), channel_id=1, source_target_pairs={{0,2},{2,4},{4,6},{6,8},{8,10},{10,12},{12,14},{14,16},{16,18},{18... | collective-permute-start | bytes 98312 | tf_op jit(solution)/shard_map/ppermute | solution.py:15
  69.4 1.3 collective-permute-start.3
  70.8 1.6 collective-permute-done.3
  74.2 0.6 convert_bitcast_fusion
  76.0 4.8 %collective-permute-start.4 = (bf16[1,128]{1,0:T(2,128)(2,1)S(1)}, bf16[1,128]{1,0:T(2,128)(2,1)S(1)}, u32[]{:S(2)}, u32[]{:S(2)}) collective-permute-start(bf16[1,128]{1,0:T(2,128)(2,1)S(1)} %get-tuple-element.87), channel_id=1, source_target_pairs={{0,2},{2,4},{4,6},{6,8},{8,10},{10,12},{12,14},{14,16},{16,18},{18... | collective-permute-start | bytes 776 | tf_op jit(solution)/shard_map/ppermute | solution.py:15
  80.8 1.3 collective-permute-start.5
  82.4 1.4 collective-permute-done.5
  84.0 1.6 multiply_convert_fusion.1
  86.1 0.3 fusion.13
  86.9 0.3 fusion.10
  87.7 0.3 fusion.8
  88.0 0.8 copy-done.3
  88.8 1.6 convert_reduce_fusion
  90.5 42.7 %all-reduce.4 = (f32[128]{0:T(128)S(1)}, f32[3,3,128]{2,1,0:T(4,128)S(1)}) all-reduce(f32[128]{0:T(128)S(1)} %convert_reduce_fusion, f32[3,3,128]{2,1,0:T(4,128)S(1)} %reshape.152), channel_id=1, replica_groups=mesh['tile'=16,'rep'=2] {'tile','rep'}, use_global_device_ids=true, to_apply=%region_11.12 | all-reduce | flops 1280 | bytes 10240 | tf_op jit(solution)/shard_map/psum | solution.py:137
  133.2 0.6 multiply_reduce_fusion.1
  134.4 0.6 multiply_reduce_fusion.2
  135.7 0.5 broadcast_divide_fusion.2
  136.3 0.6 broadcast_divide_fusion.1
  136.9 9.8 %reduce-scatter.4.cloned.1.call-done = f32[72,128]{1,0:T(8,128)} async-done(((f32[1152,128]{1,0:T(8,128)}), f32[72,128]{1,0:T(8,128)}) %reduce-scatter.4.cloned.1.call-update) | async-done | bytes 36880
  146.7 4.8 %all-gather = f32[144,128]{1,0:T(8,128)S(1)} all-gather(f32[72,128]{1,0:T(8,128)} %reduce-scatter.4.cloned.1.call-done), channel_id=2, replica_groups=mesh['tile'=16,'rep'=2] {'rep'}, dimensions={0}, use_global_device_ids=true | all-gather | bytes 110592 | tf_op jit(solution)/shard_map/all_gather | solution.py:131
  151.5 21.1 %all_gather.11 = f32[1152,128]{1,0:T(8,128)S(1)} all-gather(f32[72,128]{1,0:T(8,128)S(1)} %reduce_sum.55), channel_id=1, replica_groups=mesh['tile'=16,'rep'=2] {'tile'}, dimensions={0}, use_global_device_ids=true | all-gather | bytes 626688 | tf_op jit(solution)/shard_map/all_gather | solution.py:136
  172.7 0.7 multiply_reduce_fusion
  174.1 0.9 broadcast_divide_fusion
  (102 shorter events, 10.4 us)
Async XLA Ops:
  7.2 14.3 %copy-start = (bf16[1,512,128]{2,1,0:T(8,128)(2,1)S(1)}, bf16[1,512,128]{2,1,0:T(8,128)(2,1)}, u32[]{:S(2)}) copy-start(bf16[1,512,128]{2,1,0:T(8,128)(2,1)} %param.10) | copy-start | bytes 393220
  14.1 13.8 %all-to-all-start = ((s32[16,1,32]{2,1,0:T(1,128)}), s32[16,1,32]{2,1,0:T(1,128)S(1)}, u32[]{:S(2)}, u32[]{:S(2)}) async-start(s32[16,1,32]{2,1,0:T(1,128)} %all_to_all.11), calls=%async_computation | async-start | bytes 16384 | tf_op jit(solution)/shard_map/all_to_all | solution.py:72
  27.8 11.4 %copy-start.9 = (s32[16,1,32]{2,1,0:T(1,128)}, s32[16,1,32]{2,1,0:T(1,128)S(1)}, u32[]{:S(2)}) copy-start(s32[16,1,32]{2,1,0:T(1,128)S(1)} %all-to-all-done) | copy-start | bytes 6148
  27.8 11.4 %all-to-all-start.1 = ((bf16[16,32,128]{2,1,0:T(8,128)(2,1)}), bf16[16,32,128]{2,1,0:T(8,128)(2,1)S(1)}, u32[]{:S(2)}, u32[]{:S(2)}) async-start(bf16[16,32,128]{2,1,0:T(8,128)(2,1)} %bitcast.12), calls=%async_computation.1 | async-start | bytes 262144 | tf_op jit(solution)/shard_map/all_to_all | solution.py:69
  31.4 115.3 %reduce-scatter.4.cloned.1.call-start = ((), (), s32[]{:S(2)}) async-start(), calls=%async_computation.3 | async-start | bytes 626688
  39.3 14.9 %copy-start.10 = (bf16[3,3,128]{2,1,0:T(4,128)(2,1)S(1)}, bf16[3,3,128]{2,1,0:T(4,128)(2,1)}, u32[]{:S(2)}) copy-start(bf16[3,3,128]{2,1,0:T(4,128)(2,1)} %param.16) | copy-start | bytes 6916
  51.5 3.9 %collective-permute-start = (bf16[2,128,128]{1,2,0:T(8,128)(2,1)S(1)}, bf16[2,128,128]{1,2,0:T(8,128)(2,1)S(1)}, u32[]{:S(2)}, u32[]{:S(2)}) collective-permute-start(bf16[2,128,128]{1,2,0:T(8,128)(2,1)S(1)} %get-tuple-element.57), channel_id=1, source_target_pairs={{0,2},{2,4},{4,6},{6,8},{8,10},{10,12},{12,14},{14,16},{16,18},{18... | collective-permute-start | bytes 196616 | tf_op jit(solution)/shard_map/ppermute | solution.py:15
  52.8 3.1 %collective-permute-start.1 = (bf16[2,128,128]{1,2,0:T(8,128)(2,1)S(1)}, bf16[2,128,128]{1,2,0:T(8,128)(2,1)S(1)}, u32[]{:S(2)}, u32[]{:S(2)}) collective-permute-start(bf16[2,128,128]{1,2,0:T(8,128)(2,1)S(1)} %get-tuple-element.58), channel_id=1, source_target_pairs={{2,0},{4,2},{6,4},{8,6},{10,8},{12,10},{14,12},{16,14},{18,16},{20... | collective-permute-start | bytes 196616 | tf_op jit(solution)/shard_map/ppermute | solution.py:18
  55.4 0.6 copy-start.6
  56.0 0.6 copy-start.4
  61.0 1.3 copy-start.2
  61.2 1.1 copy-start.8
  62.3 1.0 copy-start.1
  65.0 5.9 %collective-permute-start.2 = (bf16[1,128,128]{2,1,0:T(8,128)(2,1)S(1)}, bf16[1,128,128]{2,1,0:T(8,128)(2,1)S(1)}, u32[]{:S(2)}, u32[]{:S(2)}) collective-permute-start(bf16[1,128,128]{2,1,0:T(8,128)(2,1)S(1)} %get-tuple-element.53), channel_id=1, source_target_pairs={{0,2},{2,4},{4,6},{6,8},{8,10},{10,12},{12,14},{14,16},{16,18},{18... | collective-permute-start | bytes 98312 | tf_op jit(solution)/shard_map/ppermute | solution.py:15
  69.4 3.1 %collective-permute-start.3 = (bf16[1,128,128]{2,1,0:T(8,128)(2,1)S(1)}, bf16[1,128,128]{2,1,0:T(8,128)(2,1)S(1)}, u32[]{:S(2)}, u32[]{:S(2)}) collective-permute-start(bf16[1,128,128]{2,1,0:T(8,128)(2,1)S(1)} %get-tuple-element.54), channel_id=1, source_target_pairs={{2,0},{4,2},{6,4},{8,6},{10,8},{12,10},{14,12},{16,14},{18,16},{20... | collective-permute-start | bytes 98312 | tf_op jit(solution)/shard_map/ppermute | solution.py:18
  73.5 0.7 copy-start.17
  75.8 8.2 %copy-start.11 = (f32[128]{0:T(128)S(1)}, f32[128]{0:T(128)}, u32[]{:S(2)}) copy-start(f32[128]{0:T(128)} %get-tuple-element.74) | copy-start | bytes 1540
  75.8 8.2 %copy-start.12 = (f32[128]{0:T(128)S(1)}, f32[128]{0:T(128)}, u32[]{:S(2)}) copy-start(f32[128]{0:T(128)} %get-tuple-element.75) | copy-start | bytes 1540
  75.8 8.2 %copy-start.13 = (f32[128]{0:T(128)S(1)}, f32[128]{0:T(128)}, u32[]{:S(2)}) copy-start(f32[128]{0:T(128)} %get-tuple-element.76) | copy-start | bytes 1540
  75.8 8.2 %copy-start.14 = (f32[128]{0:T(128)S(1)}, f32[128]{0:T(128)}, u32[]{:S(2)}) copy-start(f32[128]{0:T(128)} %get-tuple-element.77) | copy-start | bytes 1540
  75.8 8.2 %copy-start.15 = (f32[128]{0:T(128)S(1)}, f32[128]{0:T(128)}, u32[]{:S(2)}) copy-start(f32[128]{0:T(128)} %get-tuple-element.78) | copy-start | bytes 1540
  75.8 8.2 %copy-start.16 = (f32[128]{0:T(128)S(1)}, f32[128]{0:T(128)}, u32[]{:S(2)}) copy-start(f32[128]{0:T(128)} %get-tuple-element.79) | copy-start | bytes 1540
  76.0 6.5 %collective-permute-start.4 = (bf16[1,128]{1,0:T(2,128)(2,1)S(1)}, bf16[1,128]{1,0:T(2,128)(2,1)S(1)}, u32[]{:S(2)}, u32[]{:S(2)}) collective-permute-start(bf16[1,128]{1,0:T(2,128)(2,1)S(1)} %get-tuple-element.87), channel_id=1, source_target_pairs={{0,2},{2,4},{4,6},{6,8},{8,10},{10,12},{12,14},{14,16},{16,18},{18... | collective-permute-start | bytes 776 | tf_op jit(solution)/shard_map/ppermute | solution.py:15
  80.8 3.0 %collective-permute-start.5 = (bf16[1,128]{1,0:T(2,128)(2,1)S(1)}, bf16[1,128]{1,0:T(2,128)(2,1)S(1)}, u32[]{:S(2)}, u32[]{:S(2)}) collective-permute-start(bf16[1,128]{1,0:T(2,128)(2,1)S(1)} %get-tuple-element.88), channel_id=1, source_target_pairs={{2,0},{4,2},{6,4},{8,6},{10,8},{12,10},{14,12},{16,14},{18,16},{20... | collective-permute-start | bytes 776 | tf_op jit(solution)/shard_map/ppermute | solution.py:18
  82.4 3.5 %copy-start.7 = (bf16[2,128,128]{1,2,0:T(8,128)(2,1)S(1)}, bf16[2,128,128]{1,2,0:T(8,128)(2,1)}, u32[]{:S(2)}) copy-start(bf16[2,128,128]{1,2,0:T(8,128)(2,1)} %copy-done.6) | copy-start | bytes 196612
  86.6 0.8 copy-start.5
  88.0 0.8 copy-start.3
Sparse Core Ops, SparseCore 0:
  88.9 57.6 reduce-scatter.3
